TPU v7x, 32 devices: a whole 2x2x4 slice. The times are simulated.
32 devices in a mesh: slab: 8 (over z, y), plane: 4 (over x, core).
Axes of the slice: x: 2, y: 2, z: 4, core: 2. Of those that a mesh axis runs over, the one named last changes fastest.
Arguments:
- tissue_v: float32 [32, 64, 128], P('slab', 'plane'), may hold values from -4 to 4
- tissue_gates: float32 [40, 32, 64, 128], P(None, 'slab', 'plane'), may hold values from 0 to 1
- tissue_diff: float32 [32, 64, 128], P('slab', 'plane'), may hold values from 0.2 to 1
- fibre_v: float32 [128, 2048], P('slab', 'plane'), may hold values from -4 to 4
- fibre_gates: float32 [40, 128, 2048], P(None, 'slab', 'plane'), may hold values from 0 to 1
- fibre_diff: float32 [128, 2048], P('slab', 'plane'), may hold values from 0.2 to 1
- gate_half: float32 [40], replicated, may hold values from -3 to 3
- gate_rate: float32 [40], replicated, may hold values from 0.5 to 20
- gate_cond: float32 [40], replicated, may hold values from 0.01 to 0.15
- gate_rev: float32 [40], replicated, may hold values from -2 to 2
- junc_cond: float32 [8], replicated, may hold values from 0.25 to 2
- junc_fibre: int32 [131072], P(('slab', 'plane')), may hold values from 0 to 15
- junc_fcell: int32 [131072], P(('slab', 'plane')), may hold values from 0 to 511
- junc_owner: int32 [131072, 1], P(('slab', 'plane')), may hold values from 0 to 31; in each aligned block of 4096 rows (0 to 4095, 4096 to 8191, ...) at most 256 rows name the same one
- junc_tcell: int32 [131072], P(('slab', 'plane')), may hold values from 0 to 8191
- junc_class: int32 [131072], P(('slab', 'plane')), may hold values from 0 to 7
Outputs:
- tissue_out: float32 [32, 64, 128], P('slab', 'plane')
- fibre_out: float32 [128, 2048], P('slab', 'plane')
Inputs may be any that keep to these rules, and one draw needn't show every extreme that they name: `junc_owner`: among the junctions held by one device, no tissue block is named by more than 256 of them, and some block is named by exactly 256. `junc_fibre`: A fibre of the slab group of the device that holds the junction. `junc_fcell`: A cell of the holding device's share of that fibre. `junc_tcell`: numbered over the owner's block in the order z, y, x with x fastest.
All inputs are finite; a program needn't handle non-finite values.
Results may differ from a plain program's by a relative error of at most 0.00005.
Values sent between devices are 32-bit elements; how exact they have to be, the bound alone decides.
A program may use at most 64 MiB of HBM per device.

v0:
```python
import jax
import jax.numpy as jnp
from jax import lax
from jax.sharding import PartitionSpec as P

STEPS = 14


time_step = 0.1
gate_slope = 2.0


def with_halo(block, sides, width):
    for axis, dim in sides:
        count = lax.axis_size(axis)
        forward = [(i, i + 1) for i in range(count - 1)]
        backward = [(target, source) for source, target in forward]
        low = lax.ppermute(
            lax.slice_in_dim(block, block.shape[dim] - width, None, axis=dim), axis, forward
        )
        high = lax.ppermute(lax.slice_in_dim(block, 0, width, axis=dim), axis, backward)
        block = jnp.concatenate([low, block, high], axis=dim)
    return block


def membrane(voltage, gates, gate_half, gate_rate, gate_cond, gate_rev):
    gate_shape = (gates.shape[0],) + (1,) * (gates.ndim - 1)
    gate_signs = (
        jnp.where(jnp.arange(gates.shape[0], dtype=jnp.int32) % 2 == 0, 1.0, -1.0)
        .astype(jnp.float32)
        .reshape(gate_shape)
    )
    shifted = voltage[None] - gate_half.reshape(gate_shape)
    steady = jax.nn.sigmoid(gate_signs * gate_slope * shifted)
    decay_factor = jnp.exp(
        -time_step * gate_rate.reshape(gate_shape) * (1.0 + jax.nn.sigmoid(shifted))
    )
    renewed = steady + (gates - steady) * decay_factor
    conduct = jnp.tensordot(gate_cond, renewed, axes=1, precision=lax.Precision.HIGHEST)
    driven = jnp.tensordot(gate_cond * gate_rev, renewed, axes=1, precision=lax.Precision.HIGHEST)
    return (renewed, voltage * conduct - driven)


def line_count(length, offset, total):
    places = offset + jnp.arange(length, dtype=jnp.int32)
    return (places > 0).astype(jnp.float32) + (places < total - 1).astype(jnp.float32)


def class_gain(classes, junc_cond):
    return jnp.sum(
        jnp.where(
            classes[:, None] == jnp.arange(junc_cond.shape[0], dtype=jnp.int32)[None, :],
            junc_cond[None, :],
            jnp.zeros((), jnp.float32),
        ),
        axis=1,
    )


def make_onehot(indices, count):
    return (indices[:, None] == jnp.arange(count, dtype=jnp.int32)[None, :]).astype(jnp.float32)


def pick_values(row_onehot, col_onehot, table):
    rows_read = jnp.dot(
        row_onehot, table, precision=lax.Precision.HIGHEST, preferred_element_type=jnp.float32
    )
    return jnp.sum(rows_read * col_onehot, axis=1)


def place_values(row_onehot, col_onehot, values):
    weighted = col_onehot * values[:, None]
    return lax.dot_general(
        row_onehot,
        weighted,
        (((0,), (0,)), ((), ())),
        precision=lax.Precision.HIGHEST,
        preferred_element_type=jnp.float32,
    )


def trade_both(paired):
    return lax.all_to_all(paired, ("slab", "plane"), split_axis=1, concat_axis=1, tiled=True)


def body(
    tissue_v,
    tissue_gates,
    tissue_diff,
    fibre_v,
    fibre_gates,
    fibre_diff,
    gate_half,
    gate_rate,
    gate_cond,
    gate_rev,
    junc_cond,
    junc_fibre,
    junc_fcell,
    junc_owner,
    junc_tcell,
    junc_class,
):
    slab_count = lax.axis_size("slab")
    plane_count = lax.axis_size("plane")
    devices = slab_count * plane_count
    layers_dev, rows_dev, cols_dev = tissue_v.shape
    fibre_rows, fibre_cols = fibre_v.shape
    junctions = junc_fibre.shape[0]
    capacity = 2 * junctions // devices
    tissue_count = (
        line_count(layers_dev, lax.axis_index("slab") * layers_dev, layers_dev * slab_count)[
            :, None, None
        ]
        + line_count(rows_dev, lax.axis_index("plane") * rows_dev, rows_dev * plane_count)[
            None, :, None
        ]
        + line_count(cols_dev, 0, cols_dev)[None, None, :]
    )
    fibre_count = line_count(
        fibre_cols, lax.axis_index("plane") * fibre_cols, fibre_cols * plane_count
    )[None, :]
    fibre_cells = fibre_rows * fibre_cols
    fibre_width = 128
    fibre_grid_rows = fibre_cells // fibre_width
    tissue_grid_rows = layers_dev * rows_dev
    owners = junc_owner[:, 0]
    owner_onehot = make_onehot(owners, devices)
    owner_table = owner_onehot.astype(jnp.int32)
    slot_rank = jnp.sum(jnp.cumsum(owner_table, axis=0) * owner_table, axis=1) - 1
    rank_onehot = make_onehot(slot_rank, capacity)
    slot_index = owners * capacity + slot_rank
    fibre_index = junc_fibre * fibre_cols + junc_fcell
    fibre_row_onehot = make_onehot(fibre_index // fibre_width, fibre_grid_rows)
    fibre_col_onehot = make_onehot(fibre_index % fibre_width, fibre_width)
    cell_table = jnp.zeros((devices * capacity,), jnp.int32).at[slot_index].set(junc_tcell)
    class_table = jnp.full((devices * capacity,), -1, jnp.int32).at[slot_index].set(junc_class)
    sent_tables = jnp.stack([cell_table, class_table]).reshape(2, devices, capacity)
    got_tables = lax.all_to_all(
        sent_tables, ("slab", "plane"), split_axis=1, concat_axis=1, tiled=True
    )
    remote_cells = got_tables[0].reshape(-1)
    remote_gain = class_gain(got_tables[1].reshape(-1), junc_cond)
    own_gain = class_gain(junc_class, junc_cond)
    cell_row_onehot = make_onehot(remote_cells // cols_dev, tissue_grid_rows)
    cell_col_onehot = make_onehot(remote_cells % cols_dev, cols_dev)

    def advance(step_index, carry):
        tissue_now, tissue_state, fibre_now, fibre_state = carry
        fibre_grid = fibre_now.reshape(fibre_grid_rows, fibre_width)
        tissue_grid = tissue_now.reshape(tissue_grid_rows, cols_dev)
        fibre_at_junction = pick_values(fibre_row_onehot, fibre_col_onehot, fibre_grid)
        outgoing = place_values(owner_onehot, rank_onehot, fibre_at_junction)
        tissue_at_slot = pick_values(cell_row_onehot, cell_col_onehot, tissue_grid)
        paired = jnp.stack([outgoing, tissue_at_slot.reshape(devices, capacity)])
        traded = trade_both(paired)
        current = remote_gain * (traded[0].reshape(-1) - tissue_at_slot)
        fibre_current = own_gain * (
            fibre_at_junction - pick_values(owner_onehot, rank_onehot, traded[1])
        )
        tissue_source = place_values(cell_row_onehot, cell_col_onehot, current).reshape(
            tissue_now.shape
        )
        fibre_source = place_values(fibre_row_onehot, fibre_col_onehot, fibre_current).reshape(
            fibre_now.shape
        )
        padded = with_halo(tissue_now, (("slab", 0), ("plane", 1)), 1)
        sides = jnp.pad(tissue_now, ((0, 0), (0, 0), (1, 1)))
        neighbours = (
            padded[2:, 1:-1]
            + padded[:-2, 1:-1]
            + padded[1:-1, 2:]
            + padded[1:-1, :-2]
            + sides[:, :, 2:]
            + sides[:, :, :-2]
        )
        tissue_lap = neighbours - tissue_count * tissue_now
        fibre_padded = with_halo(fibre_now, (("plane", 1),), 1)
        fibre_lap = fibre_padded[:, 2:] + fibre_padded[:, :-2] - fibre_count * fibre_now
        tissue_state, tissue_ionic = membrane(
            tissue_now, tissue_state, gate_half, gate_rate, gate_cond, gate_rev
        )
        fibre_state, fibre_ionic = membrane(
            fibre_now, fibre_state, gate_half, gate_rate, gate_cond, gate_rev
        )
        tissue_next = tissue_now + time_step * (
            tissue_diff * tissue_lap - tissue_ionic + tissue_source
        )
        fibre_next = fibre_now + time_step * (fibre_diff * fibre_lap - fibre_ionic - fibre_source)
        return (tissue_next, tissue_state, fibre_next, fibre_state)

    final = lax.fori_loop(0, STEPS, advance, (tissue_v, tissue_gates, fibre_v, fibre_gates))
    return (final[0], final[2])


def solution(mesh):
    in_specs = (
        P("slab", "plane", None),
        P(None, "slab", "plane", None),
        P("slab", "plane", None),
        P("slab", "plane"),
        P(None, "slab", "plane"),
        P("slab", "plane"),
        P(),
        P(),
        P(),
        P(),
        P(),
        P(("slab", "plane")),
        P(("slab", "plane")),
        P(("slab", "plane"), None),
        P(("slab", "plane")),
        P(("slab", "plane")),
    )
    out_specs = (P("slab", "plane", None), P("slab", "plane"))
    return jax.shard_map(body, mesh=mesh, in_specs=in_specs, out_specs=out_specs, check_vma=False)
```

profile of v0, /device:TPU:1, one launch (start us, length us, event | category | flops | bytes accessed | tf_op | source)
XLA Modules:
  0.0 832.0 jit_solution(16049533087036332078)
XLA Ops:
  1.4 9.2 %reduce-window.6 = s32[32,32,128]{2,1,0:T(8,128)S(1)} reduce-window(s32[32,32,128]{2,1,0:T(8,128)S(1)} %convert_convert_fusion, s32[]{:T(128)} %copy.91), window={size=1x1x128 pad=0_0x0_0x127_0}, to_apply=%region_0.0 | reduce-window | flops 16646144 | bytes 1048580 | tf_op jit(solution)/shard_map/reduce-window
  12.5 15.7 %scatter_custom_fusion = s32[8192]{0:T(1024)S(1)} fusion(s32[4096]{0:T(1024)S(1)} %bitcast.127, s32[4096]{0:T(1024)} %param.32, s32[]{:T(128)} %copy.91), kind=kCustom, calls=%fused_computation.168 | custom fusion | bytes 33280 | tf_op jit(solution)/shard_map/scatter | solution.py:136
  28.2 15.5 %scatter_custom_fusion.1 = s32[8192]{0:T(1024)S(1)} fusion(s32[4096]{0:T(1024)S(1)} %bitcast.128, s32[4096]{0:T(1024)S(1)} %copy-done.11, s32[]{:T(128)} %constant.147.clone.1), kind=kCustom, calls=%fused_computation.166 | custom fusion | bytes 32772 | tf_op jit(solution)/shard_map/scatter | solution.py:137
  44.5 7.1 all-to-all-start.1
  51.7 7.1 all-to-all-done.1
  59.2 772.2 %while.19 = (s32[]{:T(128)}, f32[4,16,128]{2,1,0:T(8,128)S(1)}, f32[40,4,16,128]{3,2,1,0:T(8,128)S(1)}, f32[16,512]{1,0:T(8,128)S(1)}, f32[40,16,512]{2,1,0:T(8,...) while((s32[]{:T(128)}, f32[4,16,128]{2,1,0:T(8,128)S(1)}, ...), condition=%wide.region_11.12_spmd.clone, body=%wide.region_7.11_spmd.clone.sunk | while | flops 3262533120 | bytes 13092993 | solution.py:192
  67.8 4.1 fusion.200
  79.1 5.3 all-to-all-start
  106.3 4.6 fusion.204
  121.4 4.1 fusion.200
  132.7 7.1 all-to-all-start
  161.7 4.6 fusion.204
  176.8 4.1 fusion.200
  188.1 7.1 all-to-all-start
  217.1 4.6 fusion.204
  232.2 4.1 fusion.200
  243.6 7.1 all-to-all-start
  272.5 4.6 fusion.204
  287.6 4.1 fusion.200
  299.0 7.1 all-to-all-start
  327.9 4.6 fusion.204
  343.0 4.1 fusion.200
  354.4 7.1 all-to-all-start
  383.3 4.6 fusion.204
  398.4 4.1 fusion.200
  409.8 7.1 all-to-all-start
  438.7 4.6 fusion.204
  453.9 4.1 fusion.200
  465.2 7.1 all-to-all-start
  494.2 4.6 fusion.204
  509.3 4.1 fusion.200
  520.6 7.1 all-to-all-start
  549.6 4.6 fusion.204
  564.7 4.1 fusion.200
  576.0 7.1 all-to-all-start
  605.0 4.6 fusion.204
  620.1 4.1 fusion.200
  631.4 7.1 all-to-all-start
  660.4 4.6 fusion.204
  675.5 4.1 fusion.200
  686.8 7.1 all-to-all-start
  715.8 4.6 fusion.204
  730.9 4.1 fusion.200
  742.2 7.1 all-to-all-start
  771.2 4.6 fusion.204
  786.3 4.1 fusion.200
  797.7 7.1 all-to-all-start
  826.6 4.6 fusion.204
  (653 shorter events, 552.0 us)
Async XLA Ops:
  62.9 43.2 %collective-permute-start.4 = (f32[16,1]{1,0:T(8,128)S(1)}, f32[16,1]{1,0:T(8,128)S(1)}, u32[]{:S(2)}, u32[]{:S(2)}) collective-permute-start(f32[16,1]{1,0:T(8,128)S(1)} %get-tuple-element.541), channel_id=1, source_target_pairs={{0,1},{1,2},{2,3},{4,5},{5,6},{6,7},{8,9},{9,10},{10,11},{12,13},{... | collective-permute-start | bytes 200 | tf_op jit(solution)/shard_map/while/body/eval_jaxpr/ppermute | solution.py:18
  65.9 40.3 %collective-permute-start.5 = (f32[16,1]{1,0:T(8,128)S(1)}, f32[16,1]{1,0:T(8,128)S(1)}, u32[]{:S(2)}, u32[]{:S(2)}) collective-permute-start(f32[16,1]{1,0:T(8,128)S(1)} %get-tuple-element.542), channel_id=1, source_target_pairs={{1,0},{2,1},{3,2},{5,4},{6,5},{7,6},{9,8},{10,9},{11,10},{13,12},{... | collective-permute-start | bytes 200 | tf_op jit(solution)/shard_map/while/body/eval_jaxpr/ppermute | solution.py:21
  111.0 37.4 %collective-permute-start = (f32[1,16,128]{2,1,0:T(8,128)S(1)}, f32[1,16,128]{2,1,0:T(8,128)S(1)}, u32[]{:S(2)}, u32[]{:S(2)}) collective-permute-start(f32[1,16,128]{2,1,0:T(8,128)S(1)} %get-tuple-element.534), channel_id=1, source_target_pairs={{0,4},{4,8},{8,12},{12,16},{16,20},{20,24},{24,28},{1,5},{5,9},{9,... | collective-permute-start | bytes 24584 | tf_op jit(solution)/shard_map/while/body/eval_jaxpr/ppermute | solution.py:18
  114.1 34.3 %collective-permute-start.1 = (f32[1,16,128]{2,1,0:T(8,128)S(1)}, f32[1,16,128]{2,1,0:T(8,128)S(1)}, u32[]{:S(2)}, u32[]{:S(2)}) collective-permute-start(f32[1,16,128]{2,1,0:T(8,128)S(1)} %get-tuple-element.535), channel_id=1, source_target_pairs={{4,0},{8,4},{12,8},{16,12},{20,16},{24,20},{28,24},{5,1},{9,5},{13... | collective-permute-start | bytes 24584 | tf_op jit(solution)/shard_map/while/body/eval_jaxpr/ppermute | solution.py:21
  115.5 46.0 %collective-permute-start.4 = (f32[16,1]{1,0:T(8,128)S(1)}, f32[16,1]{1,0:T(8,128)S(1)}, u32[]{:S(2)}, u32[]{:S(2)}) collective-permute-start(f32[16,1]{1,0:T(8,128)S(1)} %get-tuple-element.541), channel_id=1, source_target_pairs={{0,1},{1,2},{2,3},{4,5},{5,6},{6,7},{8,9},{9,10},{10,11},{12,13},{... | collective-permute-start | bytes 200 | tf_op jit(solution)/shard_map/while/body/eval_jaxpr/ppermute | solution.py:18
  119.5 42.1 %collective-permute-start.5 = (f32[16,1]{1,0:T(8,128)S(1)}, f32[16,1]{1,0:T(8,128)S(1)}, u32[]{:S(2)}, u32[]{:S(2)}) collective-permute-start(f32[16,1]{1,0:T(8,128)S(1)} %get-tuple-element.542), channel_id=1, source_target_pairs={{1,0},{2,1},{3,2},{5,4},{6,5},{7,6},{9,8},{10,9},{11,10},{13,12},{... | collective-permute-start | bytes 200 | tf_op jit(solution)/shard_map/while/body/eval_jaxpr/ppermute | solution.py:21
  166.5 37.4 %collective-permute-start = (f32[1,16,128]{2,1,0:T(8,128)S(1)}, f32[1,16,128]{2,1,0:T(8,128)S(1)}, u32[]{:S(2)}, u32[]{:S(2)}) collective-permute-start(f32[1,16,128]{2,1,0:T(8,128)S(1)} %get-tuple-element.534), channel_id=1, source_target_pairs={{0,4},{4,8},{8,12},{12,16},{16,20},{20,24},{24,28},{1,5},{5,9},{9,... | collective-permute-start | bytes 24584 | tf_op jit(solution)/shard_map/while/body/eval_jaxpr/ppermute | solution.py:18
  169.6 34.3 %collective-permute-start.1 = (f32[1,16,128]{2,1,0:T(8,128)S(1)}, f32[1,16,128]{2,1,0:T(8,128)S(1)}, u32[]{:S(2)}, u32[]{:S(2)}) collective-permute-start(f32[1,16,128]{2,1,0:T(8,128)S(1)} %get-tuple-element.535), channel_id=1, source_target_pairs={{4,0},{8,4},{12,8},{16,12},{20,16},{24,20},{28,24},{5,1},{9,5},{13... | collective-permute-start | bytes 24584 | tf_op jit(solution)/shard_map/while/body/eval_jaxpr/ppermute | solution.py:21
  170.9 46.0 %collective-permute-start.4 = (f32[16,1]{1,0:T(8,128)S(1)}, f32[16,1]{1,0:T(8,128)S(1)}, u32[]{:S(2)}, u32[]{:S(2)}) collective-permute-start(f32[16,1]{1,0:T(8,128)S(1)} %get-tuple-element.541), channel_id=1, source_target_pairs={{0,1},{1,2},{2,3},{4,5},{5,6},{6,7},{8,9},{9,10},{10,11},{12,13},{... | collective-permute-start | bytes 200 | tf_op jit(solution)/shard_map/while/body/eval_jaxpr/ppermute | solution.py:18
  174.9 42.1 %collective-permute-start.5 = (f32[16,1]{1,0:T(8,128)S(1)}, f32[16,1]{1,0:T(8,128)S(1)}, u32[]{:S(2)}, u32[]{:S(2)}) collective-permute-start(f32[16,1]{1,0:T(8,128)S(1)} %get-tuple-element.542), channel_id=1, source_target_pairs={{1,0},{2,1},{3,2},{5,4},{6,5},{7,6},{9,8},{10,9},{11,10},{13,12},{... | collective-permute-start | bytes 200 | tf_op jit(solution)/shard_map/while/body/eval_jaxpr/ppermute | solution.py:21
  221.9 37.4 %collective-permute-start = (f32[1,16,128]{2,1,0:T(8,128)S(1)}, f32[1,16,128]{2,1,0:T(8,128)S(1)}, u32[]{:S(2)}, u32[]{:S(2)}) collective-permute-start(f32[1,16,128]{2,1,0:T(8,128)S(1)} %get-tuple-element.534), channel_id=1, source_target_pairs={{0,4},{4,8},{8,12},{12,16},{16,20},{20,24},{24,28},{1,5},{5,9},{9,... | collective-permute-start | bytes 24584 | tf_op jit(solution)/shard_map/while/body/eval_jaxpr/ppermute | solution.py:18
  225.0 34.3 %collective-permute-start.1 = (f32[1,16,128]{2,1,0:T(8,128)S(1)}, f32[1,16,128]{2,1,0:T(8,128)S(1)}, u32[]{:S(2)}, u32[]{:S(2)}) collective-permute-start(f32[1,16,128]{2,1,0:T(8,128)S(1)} %get-tuple-element.535), channel_id=1, source_target_pairs={{4,0},{8,4},{12,8},{16,12},{20,16},{24,20},{28,24},{5,1},{9,5},{13... | collective-permute-start | bytes 24584 | tf_op jit(solution)/shard_map/while/body/eval_jaxpr/ppermute | solution.py:21
  226.4 46.0 %collective-permute-start.4 = (f32[16,1]{1,0:T(8,128)S(1)}, f32[16,1]{1,0:T(8,128)S(1)}, u32[]{:S(2)}, u32[]{:S(2)}) collective-permute-start(f32[16,1]{1,0:T(8,128)S(1)} %get-tuple-element.541), channel_id=1, source_target_pairs={{0,1},{1,2},{2,3},{4,5},{5,6},{6,7},{8,9},{9,10},{10,11},{12,13},{... | collective-permute-start | bytes 200 | tf_op jit(solution)/shard_map/while/body/eval_jaxpr/ppermute | solution.py:18
  230.3 42.1 %collective-permute-start.5 = (f32[16,1]{1,0:T(8,128)S(1)}, f32[16,1]{1,0:T(8,128)S(1)}, u32[]{:S(2)}, u32[]{:S(2)}) collective-permute-start(f32[16,1]{1,0:T(8,128)S(1)} %get-tuple-element.542), channel_id=1, source_target_pairs={{1,0},{2,1},{3,2},{5,4},{6,5},{7,6},{9,8},{10,9},{11,10},{13,12},{... | collective-permute-start | bytes 200 | tf_op jit(solution)/shard_map/while/body/eval_jaxpr/ppermute | solution.py:21
  277.3 37.4 %collective-permute-start = (f32[1,16,128]{2,1,0:T(8,128)S(1)}, f32[1,16,128]{2,1,0:T(8,128)S(1)}, u32[]{:S(2)}, u32[]{:S(2)}) collective-permute-start(f32[1,16,128]{2,1,0:T(8,128)S(1)} %get-tuple-element.534), channel_id=1, source_target_pairs={{0,4},{4,8},{8,12},{12,16},{16,20},{20,24},{24,28},{1,5},{5,9},{9,... | collective-permute-start | bytes 24584 | tf_op jit(solution)/shard_map/while/body/eval_jaxpr/ppermute | solution.py:18
  281.8 46.0 %collective-permute-start.4 = (f32[16,1]{1,0:T(8,128)S(1)}, f32[16,1]{1,0:T(8,128)S(1)}, u32[]{:S(2)}, u32[]{:S(2)}) collective-permute-start(f32[16,1]{1,0:T(8,128)S(1)} %get-tuple-element.541), channel_id=1, source_target_pairs={{0,1},{1,2},{2,3},{4,5},{5,6},{6,7},{8,9},{9,10},{10,11},{12,13},{... | collective-permute-start | bytes 200 | tf_op jit(solution)/shard_map/while/body/eval_jaxpr/ppermute | solution.py:18
  285.7 42.1 %collective-permute-start.5 = (f32[16,1]{1,0:T(8,128)S(1)}, f32[16,1]{1,0:T(8,128)S(1)}, u32[]{:S(2)}, u32[]{:S(2)}) collective-permute-start(f32[16,1]{1,0:T(8,128)S(1)} %get-tuple-element.542), channel_id=1, source_target_pairs={{1,0},{2,1},{3,2},{5,4},{6,5},{7,6},{9,8},{10,9},{11,10},{13,12},{... | collective-permute-start | bytes 200 | tf_op jit(solution)/shard_map/while/body/eval_jaxpr/ppermute | solution.py:21
  332.7 37.4 %collective-permute-start = (f32[1,16,128]{2,1,0:T(8,128)S(1)}, f32[1,16,128]{2,1,0:T(8,128)S(1)}, u32[]{:S(2)}, u32[]{:S(2)}) collective-permute-start(f32[1,16,128]{2,1,0:T(8,128)S(1)} %get-tuple-element.534), channel_id=1, source_target_pairs={{0,4},{4,8},{8,12},{12,16},{16,20},{20,24},{24,28},{1,5},{5,9},{9,... | collective-permute-start | bytes 24584 | tf_op jit(solution)/shard_map/while/body/eval_jaxpr/ppermute | solution.py:18
  335.8 34.3 %collective-permute-start.1 = (f32[1,16,128]{2,1,0:T(8,128)S(1)}, f32[1,16,128]{2,1,0:T(8,128)S(1)}, u32[]{:S(2)}, u32[]{:S(2)}) collective-permute-start(f32[1,16,128]{2,1,0:T(8,128)S(1)} %get-tuple-element.535), channel_id=1, source_target_pairs={{4,0},{8,4},{12,8},{16,12},{20,16},{24,20},{28,24},{5,1},{9,5},{13... | collective-permute-start | bytes 24584 | tf_op jit(solution)/shard_map/while/body/eval_jaxpr/ppermute | solution.py:21
  337.2 46.0 %collective-permute-start.4 = (f32[16,1]{1,0:T(8,128)S(1)}, f32[16,1]{1,0:T(8,128)S(1)}, u32[]{:S(2)}, u32[]{:S(2)}) collective-permute-start(f32[16,1]{1,0:T(8,128)S(1)} %get-tuple-element.541), channel_id=1, source_target_pairs={{0,1},{1,2},{2,3},{4,5},{5,6},{6,7},{8,9},{9,10},{10,11},{12,13},{... | collective-permute-start | bytes 200 | tf_op jit(solution)/shard_map/while/body/eval_jaxpr/ppermute | solution.py:18
  341.1 42.1 %collective-permute-start.5 = (f32[16,1]{1,0:T(8,128)S(1)}, f32[16,1]{1,0:T(8,128)S(1)}, u32[]{:S(2)}, u32[]{:S(2)}) collective-permute-start(f32[16,1]{1,0:T(8,128)S(1)} %get-tuple-element.542), channel_id=1, source_target_pairs={{1,0},{2,1},{3,2},{5,4},{6,5},{7,6},{9,8},{10,9},{11,10},{13,12},{... | collective-permute-start | bytes 200 | tf_op jit(solution)/shard_map/while/body/eval_jaxpr/ppermute | solution.py:21
  388.1 37.4 %collective-permute-start = (f32[1,16,128]{2,1,0:T(8,128)S(1)}, f32[1,16,128]{2,1,0:T(8,128)S(1)}, u32[]{:S(2)}, u32[]{:S(2)}) collective-permute-start(f32[1,16,128]{2,1,0:T(8,128)S(1)} %get-tuple-element.534), channel_id=1, source_target_pairs={{0,4},{4,8},{8,12},{12,16},{16,20},{20,24},{24,28},{1,5},{5,9},{9,... | collective-permute-start | bytes 24584 | tf_op jit(solution)/shard_map/while/body/eval_jaxpr/ppermute | solution.py:18
  392.6 46.0 %collective-permute-start.4 = (f32[16,1]{1,0:T(8,128)S(1)}, f32[16,1]{1,0:T(8,128)S(1)}, u32[]{:S(2)}, u32[]{:S(2)}) collective-permute-start(f32[16,1]{1,0:T(8,128)S(1)} %get-tuple-element.541), channel_id=1, source_target_pairs={{0,1},{1,2},{2,3},{4,5},{5,6},{6,7},{8,9},{9,10},{10,11},{12,13},{... | collective-permute-start | bytes 200 | tf_op jit(solution)/shard_map/while/body/eval_jaxpr/ppermute | solution.py:18
  396.5 42.1 %collective-permute-start.5 = (f32[16,1]{1,0:T(8,128)S(1)}, f32[16,1]{1,0:T(8,128)S(1)}, u32[]{:S(2)}, u32[]{:S(2)}) collective-permute-start(f32[16,1]{1,0:T(8,128)S(1)} %get-tuple-element.542), channel_id=1, source_target_pairs={{1,0},{2,1},{3,2},{5,4},{6,5},{7,6},{9,8},{10,9},{11,10},{13,12},{... | collective-permute-start | bytes 200 | tf_op jit(solution)/shard_map/while/body/eval_jaxpr/ppermute | solution.py:21
  443.5 37.4 %collective-permute-start = (f32[1,16,128]{2,1,0:T(8,128)S(1)}, f32[1,16,128]{2,1,0:T(8,128)S(1)}, u32[]{:S(2)}, u32[]{:S(2)}) collective-permute-start(f32[1,16,128]{2,1,0:T(8,128)S(1)} %get-tuple-element.534), channel_id=1, source_target_pairs={{0,4},{4,8},{8,12},{12,16},{16,20},{20,24},{24,28},{1,5},{5,9},{9,... | collective-permute-start | bytes 24584 | tf_op jit(solution)/shard_map/while/body/eval_jaxpr/ppermute | solution.py:18
  448.0 46.0 %collective-permute-start.4 = (f32[16,1]{1,0:T(8,128)S(1)}, f32[16,1]{1,0:T(8,128)S(1)}, u32[]{:S(2)}, u32[]{:S(2)}) collective-permute-start(f32[16,1]{1,0:T(8,128)S(1)} %get-tuple-element.541), channel_id=1, source_target_pairs={{0,1},{1,2},{2,3},{4,5},{5,6},{6,7},{8,9},{9,10},{10,11},{12,13},{... | collective-permute-start | bytes 200 | tf_op jit(solution)/shard_map/while/body/eval_jaxpr/ppermute | solution.py:18
  451.9 42.1 %collective-permute-start.5 = (f32[16,1]{1,0:T(8,128)S(1)}, f32[16,1]{1,0:T(8,128)S(1)}, u32[]{:S(2)}, u32[]{:S(2)}) collective-permute-start(f32[16,1]{1,0:T(8,128)S(1)} %get-tuple-element.542), channel_id=1, source_target_pairs={{1,0},{2,1},{3,2},{5,4},{6,5},{7,6},{9,8},{10,9},{11,10},{13,12},{... | collective-permute-start | bytes 200 | tf_op jit(solution)/shard_map/while/body/eval_jaxpr/ppermute | solution.py:21
  498.9 37.4 %collective-permute-start = (f32[1,16,128]{2,1,0:T(8,128)S(1)}, f32[1,16,128]{2,1,0:T(8,128)S(1)}, u32[]{:S(2)}, u32[]{:S(2)}) collective-permute-start(f32[1,16,128]{2,1,0:T(8,128)S(1)} %get-tuple-element.534), channel_id=1, source_target_pairs={{0,4},{4,8},{8,12},{12,16},{16,20},{20,24},{24,28},{1,5},{5,9},{9,... | collective-permute-start | bytes 24584 | tf_op jit(solution)/shard_map/while/body/eval_jaxpr/ppermute | solution.py:18
  502.0 34.3 %collective-permute-start.1 = (f32[1,16,128]{2,1,0:T(8,128)S(1)}, f32[1,16,128]{2,1,0:T(8,128)S(1)}, u32[]{:S(2)}, u32[]{:S(2)}) collective-permute-start(f32[1,16,128]{2,1,0:T(8,128)S(1)} %get-tuple-element.535), channel_id=1, source_target_pairs={{4,0},{8,4},{12,8},{16,12},{20,16},{24,20},{28,24},{5,1},{9,5},{13... | collective-permute-start | bytes 24584 | tf_op jit(solution)/shard_map/while/body/eval_jaxpr/ppermute | solution.py:21
  503.4 46.0 %collective-permute-start.4 = (f32[16,1]{1,0:T(8,128)S(1)}, f32[16,1]{1,0:T(8,128)S(1)}, u32[]{:S(2)}, u32[]{:S(2)}) collective-permute-start(f32[16,1]{1,0:T(8,128)S(1)} %get-tuple-element.541), channel_id=1, source_target_pairs={{0,1},{1,2},{2,3},{4,5},{5,6},{6,7},{8,9},{9,10},{10,11},{12,13},{... | collective-permute-start | bytes 200 | tf_op jit(solution)/shard_map/while/body/eval_jaxpr/ppermute | solution.py:18
  507.3 42.1 %collective-permute-start.5 = (f32[16,1]{1,0:T(8,128)S(1)}, f32[16,1]{1,0:T(8,128)S(1)}, u32[]{:S(2)}, u32[]{:S(2)}) collective-permute-start(f32[16,1]{1,0:T(8,128)S(1)} %get-tuple-element.542), channel_id=1, source_target_pairs={{1,0},{2,1},{3,2},{5,4},{6,5},{7,6},{9,8},{10,9},{11,10},{13,12},{... | collective-permute-start | bytes 200 | tf_op jit(solution)/shard_map/while/body/eval_jaxpr/ppermute | solution.py:21
  554.3 37.4 %collective-permute-start = (f32[1,16,128]{2,1,0:T(8,128)S(1)}, f32[1,16,128]{2,1,0:T(8,128)S(1)}, u32[]{:S(2)}, u32[]{:S(2)}) collective-permute-start(f32[1,16,128]{2,1,0:T(8,128)S(1)} %get-tuple-element.534), channel_id=1, source_target_pairs={{0,4},{4,8},{8,12},{12,16},{16,20},{20,24},{24,28},{1,5},{5,9},{9,... | collective-permute-start | bytes 24584 | tf_op jit(solution)/shard_map/while/body/eval_jaxpr/ppermute | solution.py:18
  557.4 34.3 %collective-permute-start.1 = (f32[1,16,128]{2,1,0:T(8,128)S(1)}, f32[1,16,128]{2,1,0:T(8,128)S(1)}, u32[]{:S(2)}, u32[]{:S(2)}) collective-permute-start(f32[1,16,128]{2,1,0:T(8,128)S(1)} %get-tuple-element.535), channel_id=1, source_target_pairs={{4,0},{8,4},{12,8},{16,12},{20,16},{24,20},{28,24},{5,1},{9,5},{13... | collective-permute-start | bytes 24584 | tf_op jit(solution)/shard_map/while/body/eval_jaxpr/ppermute | solution.py:21
  558.8 46.0 %collective-permute-start.4 = (f32[16,1]{1,0:T(8,128)S(1)}, f32[16,1]{1,0:T(8,128)S(1)}, u32[]{:S(2)}, u32[]{:S(2)}) collective-permute-start(f32[16,1]{1,0:T(8,128)S(1)} %get-tuple-element.541), channel_id=1, source_target_pairs={{0,1},{1,2},{2,3},{4,5},{5,6},{6,7},{8,9},{9,10},{10,11},{12,13},{... | collective-permute-start | bytes 200 | tf_op jit(solution)/shard_map/while/body/eval_jaxpr/ppermute | solution.py:18
  562.7 42.1 %collective-permute-start.5 = (f32[16,1]{1,0:T(8,128)S(1)}, f32[16,1]{1,0:T(8,128)S(1)}, u32[]{:S(2)}, u32[]{:S(2)}) collective-permute-start(f32[16,1]{1,0:T(8,128)S(1)} %get-tuple-element.542), channel_id=1, source_target_pairs={{1,0},{2,1},{3,2},{5,4},{6,5},{7,6},{9,8},{10,9},{11,10},{13,12},{... | collective-permute-start | bytes 200 | tf_op jit(solution)/shard_map/while/body/eval_jaxpr/ppermute | solution.py:21
  609.7 37.4 %collective-permute-start = (f32[1,16,128]{2,1,0:T(8,128)S(1)}, f32[1,16,128]{2,1,0:T(8,128)S(1)}, u32[]{:S(2)}, u32[]{:S(2)}) collective-permute-start(f32[1,16,128]{2,1,0:T(8,128)S(1)} %get-tuple-element.534), channel_id=1, source_target_pairs={{0,4},{4,8},{8,12},{12,16},{16,20},{20,24},{24,28},{1,5},{5,9},{9,... | collective-permute-start | bytes 24584 | tf_op jit(solution)/shard_map/while/body/eval_jaxpr/ppermute | solution.py:18
  614.2 46.0 %collective-permute-start.4 = (f32[16,1]{1,0:T(8,128)S(1)}, f32[16,1]{1,0:T(8,128)S(1)}, u32[]{:S(2)}, u32[]{:S(2)}) collective-permute-start(f32[16,1]{1,0:T(8,128)S(1)} %get-tuple-element.541), channel_id=1, source_target_pairs={{0,1},{1,2},{2,3},{4,5},{5,6},{6,7},{8,9},{9,10},{10,11},{12,13},{... | collective-permute-start | bytes 200 | tf_op jit(solution)/shard_map/while/body/eval_jaxpr/ppermute | solution.py:18
  618.1 42.1 %collective-permute-start.5 = (f32[16,1]{1,0:T(8,128)S(1)}, f32[16,1]{1,0:T(8,128)S(1)}, u32[]{:S(2)}, u32[]{:S(2)}) collective-permute-start(f32[16,1]{1,0:T(8,128)S(1)} %get-tuple-element.542), channel_id=1, source_target_pairs={{1,0},{2,1},{3,2},{5,4},{6,5},{7,6},{9,8},{10,9},{11,10},{13,12},{... | collective-permute-start | bytes 200 | tf_op jit(solution)/shard_map/while/body/eval_jaxpr/ppermute | solution.py:21
  665.1 37.4 %collective-permute-start = (f32[1,16,128]{2,1,0:T(8,128)S(1)}, f32[1,16,128]{2,1,0:T(8,128)S(1)}, u32[]{:S(2)}, u32[]{:S(2)}) collective-permute-start(f32[1,16,128]{2,1,0:T(8,128)S(1)} %get-tuple-element.534), channel_id=1, source_target_pairs={{0,4},{4,8},{8,12},{12,16},{16,20},{20,24},{24,28},{1,5},{5,9},{9,... | collective-permute-start | bytes 24584 | tf_op jit(solution)/shard_map/while/body/eval_jaxpr/ppermute | solution.py:18
  669.6 46.0 %collective-permute-start.4 = (f32[16,1]{1,0:T(8,128)S(1)}, f32[16,1]{1,0:T(8,128)S(1)}, u32[]{:S(2)}, u32[]{:S(2)}) collective-permute-start(f32[16,1]{1,0:T(8,128)S(1)} %get-tuple-element.541), channel_id=1, source_target_pairs={{0,1},{1,2},{2,3},{4,5},{5,6},{6,7},{8,9},{9,10},{10,11},{12,13},{... | collective-permute-start | bytes 200 | tf_op jit(solution)/shard_map/while/body/eval_jaxpr/ppermute | solution.py:18
  673.6 42.1 %collective-permute-start.5 = (f32[16,1]{1,0:T(8,128)S(1)}, f32[16,1]{1,0:T(8,128)S(1)}, u32[]{:S(2)}, u32[]{:S(2)}) collective-permute-start(f32[16,1]{1,0:T(8,128)S(1)} %get-tuple-element.542), channel_id=1, source_target_pairs={{1,0},{2,1},{3,2},{5,4},{6,5},{7,6},{9,8},{10,9},{11,10},{13,12},{... | collective-permute-start | bytes 200 | tf_op jit(solution)/shard_map/while/body/eval_jaxpr/ppermute | solution.py:21
  720.6 37.4 %collective-permute-start = (f32[1,16,128]{2,1,0:T(8,128)S(1)}, f32[1,16,128]{2,1,0:T(8,128)S(1)}, u32[]{:S(2)}, u32[]{:S(2)}) collective-permute-start(f32[1,16,128]{2,1,0:T(8,128)S(1)} %get-tuple-element.534), channel_id=1, source_target_pairs={{0,4},{4,8},{8,12},{12,16},{16,20},{20,24},{24,28},{1,5},{5,9},{9,... | collective-permute-start | bytes 24584 | tf_op jit(solution)/shard_map/while/body/eval_jaxpr/ppermute | solution.py:18
  723.7 34.3 %collective-permute-start.1 = (f32[1,16,128]{2,1,0:T(8,128)S(1)}, f32[1,16,128]{2,1,0:T(8,128)S(1)}, u32[]{:S(2)}, u32[]{:S(2)}) collective-permute-start(f32[1,16,128]{2,1,0:T(8,128)S(1)} %get-tuple-element.535), channel_id=1, source_target_pairs={{4,0},{8,4},{12,8},{16,12},{20,16},{24,20},{28,24},{5,1},{9,5},{13... | collective-permute-start | bytes 24584 | tf_op jit(solution)/shard_map/while/body/eval_jaxpr/ppermute | solution.py:21
  725.0 46.0 %collective-permute-start.4 = (f32[16,1]{1,0:T(8,128)S(1)}, f32[16,1]{1,0:T(8,128)S(1)}, u32[]{:S(2)}, u32[]{:S(2)}) collective-permute-start(f32[16,1]{1,0:T(8,128)S(1)} %get-tuple-element.541), channel_id=1, source_target_pairs={{0,1},{1,2},{2,3},{4,5},{5,6},{6,7},{8,9},{9,10},{10,11},{12,13},{... | collective-permute-start | bytes 200 | tf_op jit(solution)/shard_map/while/body/eval_jaxpr/ppermute | solution.py:18
  729.0 42.1 %collective-permute-start.5 = (f32[16,1]{1,0:T(8,128)S(1)}, f32[16,1]{1,0:T(8,128)S(1)}, u32[]{:S(2)}, u32[]{:S(2)}) collective-permute-start(f32[16,1]{1,0:T(8,128)S(1)} %get-tuple-element.542), channel_id=1, source_target_pairs={{1,0},{2,1},{3,2},{5,4},{6,5},{7,6},{9,8},{10,9},{11,10},{13,12},{... | collective-permute-start | bytes 200 | tf_op jit(solution)/shard_map/while/body/eval_jaxpr/ppermute | solution.py:21
  776.0 37.4 %collective-permute-start = (f32[1,16,128]{2,1,0:T(8,128)S(1)}, f32[1,16,128]{2,1,0:T(8,128)S(1)}, u32[]{:S(2)}, u32[]{:S(2)}) collective-permute-start(f32[1,16,128]{2,1,0:T(8,128)S(1)} %get-tuple-element.534), channel_id=1, source_target_pairs={{0,4},{4,8},{8,12},{12,16},{16,20},{20,24},{24,28},{1,5},{5,9},{9,... | collective-permute-start | bytes 24584 | tf_op jit(solution)/shard_map/while/body/eval_jaxpr/ppermute | solution.py:18
  780.5 46.0 %collective-permute-start.4 = (f32[16,1]{1,0:T(8,128)S(1)}, f32[16,1]{1,0:T(8,128)S(1)}, u32[]{:S(2)}, u32[]{:S(2)}) collective-permute-start(f32[16,1]{1,0:T(8,128)S(1)} %get-tuple-element.541), channel_id=1, source_target_pairs={{0,1},{1,2},{2,3},{4,5},{5,6},{6,7},{8,9},{9,10},{10,11},{12,13},{... | collective-permute-start | bytes 200 | tf_op jit(solution)/shard_map/while/body/eval_jaxpr/ppermute | solution.py:18
  784.4 42.1 %collective-permute-start.5 = (f32[16,1]{1,0:T(8,128)S(1)}, f32[16,1]{1,0:T(8,128)S(1)}, u32[]{:S(2)}, u32[]{:S(2)}) collective-permute-start(f32[16,1]{1,0:T(8,128)S(1)} %get-tuple-element.542), channel_id=1, source_target_pairs={{1,0},{2,1},{3,2},{5,4},{6,5},{7,6},{9,8},{10,9},{11,10},{13,12},{... | collective-permute-start | bytes 200 | tf_op jit(solution)/shard_map/while/body/eval_jaxpr/ppermute | solution.py:21
  (68 other events, 1556.7 us)
where the time goes:
time: 835 us; the launch traced here: 832 us
  matrix products  402 us (48%)
  starting transfers between devices  322 us (39%)
  other arithmetic  49.1 us (6%)
  local copies, waits for them, and re-layouts  45.3 us (5%)
    dot_general x42, matrix products, place_values(): lax.dot_general(row_onehot, weighted, (((0,), (0,)), ((), ())), precision...  167 us
    dot_general x42, matrix products, pick_values(): jnp.dot(row_onehot, table, precision=lax.Precision.HIGHEST, preferred_ele...  151 us
    ppermute x42, starting transfers between devices, with_halo(): lax.ppermute(lax.slice_in_dim(block, block.shape[dim] - width, None, axis...  146 us
    all_to_all x14, starting transfers between devices, trade_both(): lax.all_to_all(paired, ('slab', 'plane'), split_axis=1, concat_axis=1, ti...  97.8 us
    ppermute x42, starting transfers between devices, with_halo(): lax.ppermute(lax.slice_in_dim(block, 0, width, axis=dim), axis, backward)  71.9 us
    dot_general x28, matrix products, membrane(): jnp.tensordot(gate_cond, renewed, axes=1, precision=lax.Precision.HIGHEST)  42.3 us
    dot_general x28, matrix products, membrane(): jnp.tensordot(gate_cond * gate_rev, renewed, axes=1, precision=lax.Precis...  42.3 us
    add x28, other arithmetic, membrane(): renewed = steady + (gates - steady) * decay_factor  34.6 us
  transfers between devices with their start and end apart: 99, of which 1 were waited for; matrix products, arithmetic and copies ran while one was open for 54% of the time, Pallas kernels for 0%

commit v1 on v0

--- a/solution.py
+++ b/solution.py
@@ -10,17 +10,11 @@
 gate_slope = 2.0
 
 
-def with_halo(block, sides, width):
-    for axis, dim in sides:
-        count = lax.axis_size(axis)
-        forward = [(i, i + 1) for i in range(count - 1)]
-        backward = [(target, source) for source, target in forward]
-        low = lax.ppermute(
-            lax.slice_in_dim(block, block.shape[dim] - width, None, axis=dim), axis, forward
-        )
-        high = lax.ppermute(lax.slice_in_dim(block, 0, width, axis=dim), axis, backward)
-        block = jnp.concatenate([low, block, high], axis=dim)
-    return block
+def shift_pair(up, down, axis):
+    count = lax.axis_size(axis)
+    forward = [(i, i + 1) for i in range(count - 1)]
+    backward = [(target, source) for source, target in forward]
+    return lax.ppermute(up, axis, forward), lax.ppermute(down, axis, backward)
 
 
 def membrane(voltage, gates, gate_half, gate_rate, gate_cond, gate_rev):
@@ -36,9 +30,8 @@
         -time_step * gate_rate.reshape(gate_shape) * (1.0 + jax.nn.sigmoid(shifted))
     )
     renewed = steady + (gates - steady) * decay_factor
-    conduct = jnp.tensordot(gate_cond, renewed, axes=1, precision=lax.Precision.HIGHEST)
-    driven = jnp.tensordot(gate_cond * gate_rev, renewed, axes=1, precision=lax.Precision.HIGHEST)
-    return (renewed, voltage * conduct - driven)
+    driving = gate_cond.reshape(gate_shape) * (voltage[None] - gate_rev.reshape(gate_shape))
+    return (renewed, jnp.sum(driving * renewed, axis=0))
 
 
 def line_count(length, offset, total):
@@ -61,11 +54,51 @@
     return (indices[:, None] == jnp.arange(count, dtype=jnp.int32)[None, :]).astype(jnp.float32)
 
 
-def pick_values(row_onehot, col_onehot, table):
+def split_two(values):
+    high = lax.reduce_precision(values, 8, 7)
+    low = lax.reduce_precision(values - high, 8, 7)
+    return high, low
+
+
+def pick_split(rows, cols, table):
+    depth, width = table.shape
+    high, low = split_two(table)
+    stacked = jnp.concatenate([high, low], axis=0).astype(jnp.bfloat16)
+    onehot = rows[:, None] == (jnp.arange(2 * depth, dtype=jnp.int32) % depth)[None, :]
     rows_read = jnp.dot(
-        row_onehot, table, precision=lax.Precision.HIGHEST, preferred_element_type=jnp.float32
-    )
-    return jnp.sum(rows_read * col_onehot, axis=1)
+        onehot.astype(jnp.bfloat16), stacked, preferred_element_type=jnp.float32
+    )
+    chosen = cols[:, None] == jnp.arange(width, dtype=jnp.int32)[None, :]
+    return jnp.sum(jnp.where(chosen, rows_read, 0.0), axis=1)
+
+
+def place_split(rows, cols, values, depth, width):
+    high, low = split_two(values)
+    lanes = jnp.arange(2 * width, dtype=jnp.int32)
+    both = jnp.where((lanes < width)[None, :], high[:, None], low[:, None])
+    weighted = jnp.where(cols[:, None] == (lanes % width)[None, :], both, 0.0)
+    onehot = (rows[:, None] == jnp.arange(depth, dtype=jnp.int32)[None, :]).astype(jnp.bfloat16)
+    halves = lax.dot_general(
+        onehot,
+        weighted.astype(jnp.bfloat16),
+        (((0,), (0,)), ((), ())),
+        preferred_element_type=jnp.float32,
+    )
+    return halves[:, :width] + halves[:, width:]
+
+
+def running_rank(owner_onehot):
+    total, kinds = owner_onehot.shape
+    tall = 128
+    blocks = owner_onehot.astype(jnp.bfloat16).reshape(total // tall, tall, kinds)
+    lower = jnp.tril(jnp.ones((tall, tall), jnp.bfloat16))
+    within = jnp.einsum("ij,bjo->bio", lower, blocks, preferred_element_type=jnp.float32)
+    sums = within[:, -1, :]
+    count = total // tall
+    before = jnp.tril(jnp.ones((count, count), jnp.float32), -1)
+    ahead = jnp.dot(before, sums, precision=lax.Precision.HIGHEST)
+    ranks = jnp.sum((within + ahead[:, None, :]).reshape(total, kinds) * owner_onehot, axis=1)
+    return jnp.round(ranks).astype(jnp.int32) - 1
 
 
 def place_values(row_onehot, col_onehot, values):
@@ -126,57 +159,59 @@
     tissue_grid_rows = layers_dev * rows_dev
     owners = junc_owner[:, 0]
     owner_onehot = make_onehot(owners, devices)
-    owner_table = owner_onehot.astype(jnp.int32)
-    slot_rank = jnp.sum(jnp.cumsum(owner_table, axis=0) * owner_table, axis=1) - 1
-    rank_onehot = make_onehot(slot_rank, capacity)
-    slot_index = owners * capacity + slot_rank
-    fibre_index = junc_fibre * fibre_cols + junc_fcell
-    fibre_row_onehot = make_onehot(fibre_index // fibre_width, fibre_grid_rows)
-    fibre_col_onehot = make_onehot(fibre_index % fibre_width, fibre_width)
-    cell_table = jnp.zeros((devices * capacity,), jnp.int32).at[slot_index].set(junc_tcell)
-    class_table = jnp.full((devices * capacity,), -1, jnp.int32).at[slot_index].set(junc_class)
-    sent_tables = jnp.stack([cell_table, class_table]).reshape(2, devices, capacity)
+    rank_onehot = make_onehot(running_rank(owner_onehot), capacity)
+    kinds = junc_cond.shape[0] + 1
+    code = (junc_tcell * kinds + junc_class + 1).astype(jnp.float32)
+    code_table = jnp.round(place_values(owner_onehot, rank_onehot, code)).astype(jnp.int32)
+    fibre_index = (junc_fibre * fibre_cols + junc_fcell).astype(jnp.float32)
+    fibre_table = jnp.round(place_values(owner_onehot, rank_onehot, fibre_index))
+    own_cells = fibre_table.astype(jnp.int32).reshape(-1)
+    sent_tables = jnp.stack([code_table // kinds, code_table % kinds - 1])
     got_tables = lax.all_to_all(
         sent_tables, ("slab", "plane"), split_axis=1, concat_axis=1, tiled=True
     )
     remote_cells = got_tables[0].reshape(-1)
     remote_gain = class_gain(got_tables[1].reshape(-1), junc_cond)
-    own_gain = class_gain(junc_class, junc_cond)
-    cell_row_onehot = make_onehot(remote_cells // cols_dev, tissue_grid_rows)
-    cell_col_onehot = make_onehot(remote_cells % cols_dev, cols_dev)
+    own_gain = class_gain(sent_tables[1].reshape(-1), junc_cond)
+    fibre_at_row, fibre_at_col = own_cells // fibre_width, own_cells % fibre_width
+    cell_row, cell_col = remote_cells // cols_dev, remote_cells % cols_dev
 
     def advance(step_index, carry):
         tissue_now, tissue_state, fibre_now, fibre_state = carry
         fibre_grid = fibre_now.reshape(fibre_grid_rows, fibre_width)
         tissue_grid = tissue_now.reshape(tissue_grid_rows, cols_dev)
-        fibre_at_junction = pick_values(fibre_row_onehot, fibre_col_onehot, fibre_grid)
-        outgoing = place_values(owner_onehot, rank_onehot, fibre_at_junction)
-        tissue_at_slot = pick_values(cell_row_onehot, cell_col_onehot, tissue_grid)
-        paired = jnp.stack([outgoing, tissue_at_slot.reshape(devices, capacity)])
-        traded = trade_both(paired)
-        current = remote_gain * (traded[0].reshape(-1) - tissue_at_slot)
-        fibre_current = own_gain * (
-            fibre_at_junction - pick_values(owner_onehot, rank_onehot, traded[1])
-        )
-        tissue_source = place_values(cell_row_onehot, cell_col_onehot, current).reshape(
-            tissue_now.shape
-        )
-        fibre_source = place_values(fibre_row_onehot, fibre_col_onehot, fibre_current).reshape(
-            fibre_now.shape
-        )
-        padded = with_halo(tissue_now, (("slab", 0), ("plane", 1)), 1)
+        end_pad = (0, cols_dev - fibre_rows)
+        up = jnp.concatenate([tissue_now[:, -1], jnp.pad(fibre_now[:, -1], end_pad)[None]])
+        down = jnp.concatenate([tissue_now[:, 0], jnp.pad(fibre_now[:, 0], end_pad)[None]])
+        y_low, y_high = shift_pair(up, down, "plane")
+        z_low, z_high = shift_pair(tissue_now[-1:], tissue_now[:1], "slab")
+        fibre_at_slot = pick_split(fibre_at_row, fibre_at_col, fibre_grid)
+        tissue_at_slot = pick_split(cell_row, cell_col, tissue_grid)
+        paired = jnp.stack([fibre_at_slot, tissue_at_slot]).reshape(2, devices, capacity)
+        traded = trade_both(paired).reshape(2, -1)
+        current = remote_gain * (traded[0] - tissue_at_slot)
+        fibre_current = own_gain * (fibre_at_slot - traded[1])
+        tissue_source = place_split(
+            cell_row, cell_col, current, tissue_grid_rows, cols_dev
+        ).reshape(tissue_now.shape)
+        fibre_source = place_split(
+            fibre_at_row, fibre_at_col, fibre_current, fibre_grid_rows, fibre_width
+        ).reshape(fibre_now.shape)
         sides = jnp.pad(tissue_now, ((0, 0), (0, 0), (1, 1)))
         neighbours = (
-            padded[2:, 1:-1]
-            + padded[:-2, 1:-1]
-            + padded[1:-1, 2:]
-            + padded[1:-1, :-2]
+            jnp.concatenate([tissue_now[1:], z_high], axis=0)
+            + jnp.concatenate([z_low, tissue_now[:-1]], axis=0)
+            + jnp.concatenate([tissue_now[:, 1:], y_high[:-1, None]], axis=1)
+            + jnp.concatenate([y_low[:-1, None], tissue_now[:, :-1]], axis=1)
             + sides[:, :, 2:]
             + sides[:, :, :-2]
         )
         tissue_lap = neighbours - tissue_count * tissue_now
-        fibre_padded = with_halo(fibre_now, (("plane", 1),), 1)
-        fibre_lap = fibre_padded[:, 2:] + fibre_padded[:, :-2] - fibre_count * fibre_now
+        fibre_lap = (
+            jnp.concatenate([fibre_now[:, 1:], y_high[-1, :fibre_rows, None]], axis=1)
+            + jnp.concatenate([y_low[-1, :fibre_rows, None], fibre_now[:, :-1]], axis=1)
+            - fibre_count * fibre_now
+        )
         tissue_state, tissue_ionic = membrane(
             tissue_now, tissue_state, gate_half, gate_rate, gate_cond, gate_rev
         )

time: 835 us -> 496 us (0.59)
  matrix products: 402 us -> 164 us
  starting transfers between devices: 322 us -> 197 us
  waiting for transfers between devices: 7.37 us -> 68.3 us
  local copies, waits for them, and re-layouts: 45.3 us -> 10.2 us
    dot_general x42 -> x2, matrix products: 167 us -> 3.9 us  [place_values(): lax.dot_general(row_onehot, weighted, (((0,), (0,)), ((), ())), precision...]
    ppermute x84 -> x56, starting transfers between devices: 218 us -> 141 us  [shift_pair(): return (lax.ppermute(up, axis, forward), lax.ppermute(down, axis, backward))]
    dot_general x98 -> x58, matrix products: 235 us -> 160 us  [the longest x28 96.1 us: place_split(): lax.dot_general(onehot, weighted.astype(jnp.bfloat16), (((0,), (0,)), (()...]
    all_to_all x14, waiting for transfers between devices: 0.04 us -> 63 us  [trade_both(): lax.all_to_all(paired, ('slab', 'plane'), split_axis=1, concat_axis=1, ti...]
    all_to_all x14, starting transfers between devices: 97.8 us -> 48.8 us  [trade_both(): lax.all_to_all(paired, ('slab', 'plane'), split_axis=1, concat_axis=1, ti...]
    add x28 -> x29, other arithmetic: 34.6 us -> 0.18 us  [the longest x28 0.18 us: place_split(): return halves[:, :width] + halves[:, width:]]
    reduce_sum x1 -> x29, other arithmetic: 0.34 us -> 33.7 us  [the longest x28 33.5 us: membrane(): return (renewed, jnp.sum(driving * renewed, axis=0))]
    scatter x2 -> x0, local copies, waits for them, and re-layouts: 31.3 us -> none  [the longest x1 15.7 us: body(): jnp.zeros((devices * capacity,), jnp.int32).at[slot_index].set(junc_tcell)]
  transfers between devices with their start and end apart: 99 -> 71, of which waited for: 1 -> 15; matrix products, arithmetic and copies ran while one was open for 54% -> 43% of each run, Pallas kernels for 0% -> 0%
where the time goes in v1:
time: 496 us; the launch traced here: 494 us
  starting transfers between devices  197 us (40%)
  matrix products  164 us (33%)
  waiting for transfers between devices  68.3 us (14%)
  other arithmetic  47.9 us (10%)
  local copies, waits for them, and re-layouts  10.2 us (2%)
  loops' own time  5.33 us (1%)
    ppermute x56, starting transfers between devices, shift_pair(): return (lax.ppermute(up, axis, forward), lax.ppermute(down, axis, backward))  141 us
    dot_general x28, matrix products, place_split(): lax.dot_general(onehot, weighted.astype(jnp.bfloat16), (((0,), (0,)), (()...  96.1 us
    dot_general x28, matrix products, pick_split(): jnp.dot(onehot.astype(jnp.bfloat16), stacked, preferred_element_type=jnp....  63.1 us
    all_to_all x14, waiting for transfers between devices, trade_both(): lax.all_to_all(paired, ('slab', 'plane'), split_axis=1, concat_axis=1, ti...  63 us
    all_to_all x14, starting transfers between devices, trade_both(): lax.all_to_all(paired, ('slab', 'plane'), split_axis=1, concat_axis=1, ti...  48.8 us
    reduce_sum x28, other arithmetic, membrane(): return (renewed, jnp.sum(driving * renewed, axis=0))  33.5 us
  transfers between devices with their start and end apart: 71, of which 15 were waited for; matrix products, arithmetic and copies ran while one was open for 43% of the time, Pallas kernels for 0%

profile of v1, /device:TPU:1, one launch (start us, length us, event | category | flops | bytes accessed | tf_op | source)
XLA Modules:
  0.0 493.7 jit_solution(6374147802733579538)
XLA Ops:
  5.3 7.1 %all-to-all-start.1 = ((s32[2,32,256]{2,0,1:T(2,128)}), s32[2,32,256]{2,0,1:T(2,128)S(1)}, u32[]{:S(2)}, u32[]{:S(2)}) async-start(s32[2,32,256]{2,0,1:T(2,128)} %copy.60), calls=%async_computation.1 | async-start | bytes 131072 | tf_op jit(solution)/shard_map/all_to_all | solution.py:170
  14.5 5.1 %all-to-all-done.1 = s32[2,32,256]{2,0,1:T(2,128)S(1)} async-done(((s32[2,32,256]{2,0,1:T(2,128)}), s32[2,32,256]{2,0,1:T(2,128)S(1)}, u32[]{:S(2)}, u32[]{:S(2)}) %all-to-all-start.1) | async-done | bytes 65568 | tf_op jit(solution)/shard_map/all_to_all | solution.py:170
  20.1 472.9 %while.20 = (s32[]{:T(128)}, f32[4,16,128]{2,1,0:T(8,128)S(1)}, f32[40,4,16,128]{3,2,1,0:T(8,128)S(1)}, f32[16,512]{1,0:T(8,128)S(1)}, f32[40,16,512]{2,1,0:T(8,...) while((s32[]{:T(128)}, f32[4,16,128]{2,1,0:T(8,128)S(1)}, ...), condition=%wide.region_8.9_spmd.clone, body=%wide.region_3.8_spmd.clone.sunk | while | flops 1107442944 | bytes 8335497 | solution.py:227
  21.6 4.0 collective-permute-start.1
  36.0 3.5 all-to-all-start
  42.3 4.5 all-to-all-done
  46.8 3.4 fusion.179
  50.4 3.4 fusion.173
  55.4 4.0 collective-permute-start.1
  69.8 3.5 all-to-all-start
  76.0 4.5 all-to-all-done
  80.6 3.4 fusion.179
  89.2 4.0 collective-permute-start.1
  103.5 3.5 all-to-all-start
  109.8 4.5 all-to-all-done
  122.9 4.0 collective-permute-start.1
  137.3 3.5 all-to-all-start
  143.6 4.5 all-to-all-done
  156.7 4.0 collective-permute-start.1
  171.1 3.5 all-to-all-start
  177.3 4.5 all-to-all-done
  190.5 4.0 collective-permute-start.1
  204.8 3.5 all-to-all-start
  211.1 4.5 all-to-all-done
  224.2 4.0 collective-permute-start.1
  238.6 3.5 all-to-all-start
  244.9 4.5 all-to-all-done
  258.0 4.0 collective-permute-start.1
  272.4 3.5 all-to-all-start
  278.6 4.5 all-to-all-done
  291.8 4.0 collective-permute-start.1
  306.1 3.5 all-to-all-start
  312.4 4.5 all-to-all-done
  325.5 4.0 collective-permute-start.1
  339.9 3.5 all-to-all-start
  346.2 4.5 all-to-all-done
  359.3 4.0 collective-permute-start.1
  373.7 3.5 all-to-all-start
  379.9 4.5 all-to-all-done
  393.1 4.0 collective-permute-start.1
  407.4 3.5 all-to-all-start
  413.7 4.5 all-to-all-done
  426.8 4.0 collective-permute-start.1
  441.2 3.5 all-to-all-start
  447.5 4.5 all-to-all-done
  460.6 4.0 collective-permute-start.1
  475.0 3.5 all-to-all-start
  481.2 4.5 all-to-all-done
  (810 shorter events, 297.1 us)
Async XLA Ops:
  5.3 14.4 %all-to-all-start.1 = ((s32[2,32,256]{2,0,1:T(2,128)}), s32[2,32,256]{2,0,1:T(2,128)S(1)}, u32[]{:S(2)}, u32[]{:S(2)}) async-start(s32[2,32,256]{2,0,1:T(2,128)} %copy.60), calls=%async_computation.1 | async-start | bytes 131072 | tf_op jit(solution)/shard_map/all_to_all | solution.py:170
  20.3 33.6 %collective-permute-start = (f32[1,16,128]{2,1,0:T(8,128)S(1)}, f32[1,16,128]{2,1,0:T(8,128)S(1)}, u32[]{:S(2)}, u32[]{:S(2)}) collective-permute-start(f32[1,16,128]{2,1,0:T(8,128)S(1)} %get-tuple-element.600), channel_id=1, source_target_pairs={{4,0},{8,4},{12,8},{16,12},{20,16},{24,20},{28,24},{5,1},{9,5},{13... | collective-permute-start | bytes 24584 | tf_op jit(solution)/shard_map/while/body/eval_jaxpr/ppermute | solution.py:17
  21.6 32.3 %collective-permute-start.1 = (f32[1,16,128]{2,1,0:T(8,128)S(1)}, f32[1,16,128]{2,1,0:T(8,128)S(1)}, u32[]{:S(2)}, u32[]{:S(2)}) collective-permute-start(f32[1,16,128]{2,1,0:T(8,128)S(1)} %get-tuple-element.603), channel_id=1, source_target_pairs={{0,4},{4,8},{8,12},{12,16},{16,20},{20,24},{24,28},{1,5},{5,9},{9,... | collective-permute-start | bytes 24584 | tf_op jit(solution)/shard_map/while/body/eval_jaxpr/ppermute | solution.py:17
  25.9 16.2 %collective-permute-start.3 = (f32[5,128]{1,0:T(8,128)S(1)}, f32[5,128]{1,0:T(8,128)S(1)}, u32[]{:S(2)}, u32[]{:S(2)}) collective-permute-start(f32[5,128]{1,0:T(8,128)S(1)} %pad_maximum_fusion.8), channel_id=1, source_target_pairs={{0,1},{1,2},{2,3},{4,5},{5,6},{6,7},{8,9},{9,10},{10,11},{12,13},{... | collective-permute-start | bytes 7688 | tf_op jit(solution)/shard_map/while/body/eval_jaxpr/ppermute | solution.py:17
  28.8 13.4 %collective-permute-start.2 = (f32[5,128]{1,0:T(8,128)S(1)}, f32[5,128]{1,0:T(8,128)S(1)}, u32[]{:S(2)}, u32[]{:S(2)}) collective-permute-start(f32[5,128]{1,0:T(8,128)S(1)} %pad_maximum_fusion.7), channel_id=1, source_target_pairs={{1,0},{2,1},{3,2},{5,4},{6,5},{7,6},{9,8},{10,9},{11,10},{13,12},{... | collective-permute-start | bytes 7688 | tf_op jit(solution)/shard_map/while/body/eval_jaxpr/ppermute | solution.py:17
  54.1 33.6 %collective-permute-start = (f32[1,16,128]{2,1,0:T(8,128)S(1)}, f32[1,16,128]{2,1,0:T(8,128)S(1)}, u32[]{:S(2)}, u32[]{:S(2)}) collective-permute-start(f32[1,16,128]{2,1,0:T(8,128)S(1)} %get-tuple-element.600), channel_id=1, source_target_pairs={{4,0},{8,4},{12,8},{16,12},{20,16},{24,20},{28,24},{5,1},{9,5},{13... | collective-permute-start | bytes 24584 | tf_op jit(solution)/shard_map/while/body/eval_jaxpr/ppermute | solution.py:17
  55.4 32.3 %collective-permute-start.1 = (f32[1,16,128]{2,1,0:T(8,128)S(1)}, f32[1,16,128]{2,1,0:T(8,128)S(1)}, u32[]{:S(2)}, u32[]{:S(2)}) collective-permute-start(f32[1,16,128]{2,1,0:T(8,128)S(1)} %get-tuple-element.603), channel_id=1, source_target_pairs={{0,4},{4,8},{8,12},{12,16},{16,20},{20,24},{24,28},{1,5},{5,9},{9,... | collective-permute-start | bytes 24584 | tf_op jit(solution)/shard_map/while/body/eval_jaxpr/ppermute | solution.py:17
  59.6 16.2 %collective-permute-start.3 = (f32[5,128]{1,0:T(8,128)S(1)}, f32[5,128]{1,0:T(8,128)S(1)}, u32[]{:S(2)}, u32[]{:S(2)}) collective-permute-start(f32[5,128]{1,0:T(8,128)S(1)} %pad_maximum_fusion.8), channel_id=1, source_target_pairs={{0,1},{1,2},{2,3},{4,5},{5,6},{6,7},{8,9},{9,10},{10,11},{12,13},{... | collective-permute-start | bytes 7688 | tf_op jit(solution)/shard_map/while/body/eval_jaxpr/ppermute | solution.py:17
  62.6 13.4 %collective-permute-start.2 = (f32[5,128]{1,0:T(8,128)S(1)}, f32[5,128]{1,0:T(8,128)S(1)}, u32[]{:S(2)}, u32[]{:S(2)}) collective-permute-start(f32[5,128]{1,0:T(8,128)S(1)} %pad_maximum_fusion.7), channel_id=1, source_target_pairs={{1,0},{2,1},{3,2},{5,4},{6,5},{7,6},{9,8},{10,9},{11,10},{13,12},{... | collective-permute-start | bytes 7688 | tf_op jit(solution)/shard_map/while/body/eval_jaxpr/ppermute | solution.py:17
  87.9 33.6 %collective-permute-start = (f32[1,16,128]{2,1,0:T(8,128)S(1)}, f32[1,16,128]{2,1,0:T(8,128)S(1)}, u32[]{:S(2)}, u32[]{:S(2)}) collective-permute-start(f32[1,16,128]{2,1,0:T(8,128)S(1)} %get-tuple-element.600), channel_id=1, source_target_pairs={{4,0},{8,4},{12,8},{16,12},{20,16},{24,20},{28,24},{5,1},{9,5},{13... | collective-permute-start | bytes 24584 | tf_op jit(solution)/shard_map/while/body/eval_jaxpr/ppermute | solution.py:17
  89.2 32.3 %collective-permute-start.1 = (f32[1,16,128]{2,1,0:T(8,128)S(1)}, f32[1,16,128]{2,1,0:T(8,128)S(1)}, u32[]{:S(2)}, u32[]{:S(2)}) collective-permute-start(f32[1,16,128]{2,1,0:T(8,128)S(1)} %get-tuple-element.603), channel_id=1, source_target_pairs={{0,4},{4,8},{8,12},{12,16},{16,20},{20,24},{24,28},{1,5},{5,9},{9,... | collective-permute-start | bytes 24584 | tf_op jit(solution)/shard_map/while/body/eval_jaxpr/ppermute | solution.py:17
  93.4 16.2 %collective-permute-start.3 = (f32[5,128]{1,0:T(8,128)S(1)}, f32[5,128]{1,0:T(8,128)S(1)}, u32[]{:S(2)}, u32[]{:S(2)}) collective-permute-start(f32[5,128]{1,0:T(8,128)S(1)} %pad_maximum_fusion.8), channel_id=1, source_target_pairs={{0,1},{1,2},{2,3},{4,5},{5,6},{6,7},{8,9},{9,10},{10,11},{12,13},{... | collective-permute-start | bytes 7688 | tf_op jit(solution)/shard_map/while/body/eval_jaxpr/ppermute | solution.py:17
  96.3 13.4 %collective-permute-start.2 = (f32[5,128]{1,0:T(8,128)S(1)}, f32[5,128]{1,0:T(8,128)S(1)}, u32[]{:S(2)}, u32[]{:S(2)}) collective-permute-start(f32[5,128]{1,0:T(8,128)S(1)} %pad_maximum_fusion.7), channel_id=1, source_target_pairs={{1,0},{2,1},{3,2},{5,4},{6,5},{7,6},{9,8},{10,9},{11,10},{13,12},{... | collective-permute-start | bytes 7688 | tf_op jit(solution)/shard_map/while/body/eval_jaxpr/ppermute | solution.py:17
  121.6 33.6 %collective-permute-start = (f32[1,16,128]{2,1,0:T(8,128)S(1)}, f32[1,16,128]{2,1,0:T(8,128)S(1)}, u32[]{:S(2)}, u32[]{:S(2)}) collective-permute-start(f32[1,16,128]{2,1,0:T(8,128)S(1)} %get-tuple-element.600), channel_id=1, source_target_pairs={{4,0},{8,4},{12,8},{16,12},{20,16},{24,20},{28,24},{5,1},{9,5},{13... | collective-permute-start | bytes 24584 | tf_op jit(solution)/shard_map/while/body/eval_jaxpr/ppermute | solution.py:17
  122.9 32.3 %collective-permute-start.1 = (f32[1,16,128]{2,1,0:T(8,128)S(1)}, f32[1,16,128]{2,1,0:T(8,128)S(1)}, u32[]{:S(2)}, u32[]{:S(2)}) collective-permute-start(f32[1,16,128]{2,1,0:T(8,128)S(1)} %get-tuple-element.603), channel_id=1, source_target_pairs={{0,4},{4,8},{8,12},{12,16},{16,20},{20,24},{24,28},{1,5},{5,9},{9,... | collective-permute-start | bytes 24584 | tf_op jit(solution)/shard_map/while/body/eval_jaxpr/ppermute | solution.py:17
  127.2 16.2 %collective-permute-start.3 = (f32[5,128]{1,0:T(8,128)S(1)}, f32[5,128]{1,0:T(8,128)S(1)}, u32[]{:S(2)}, u32[]{:S(2)}) collective-permute-start(f32[5,128]{1,0:T(8,128)S(1)} %pad_maximum_fusion.8), channel_id=1, source_target_pairs={{0,1},{1,2},{2,3},{4,5},{5,6},{6,7},{8,9},{9,10},{10,11},{12,13},{... | collective-permute-start | bytes 7688 | tf_op jit(solution)/shard_map/while/body/eval_jaxpr/ppermute | solution.py:17
  155.4 33.6 %collective-permute-start = (f32[1,16,128]{2,1,0:T(8,128)S(1)}, f32[1,16,128]{2,1,0:T(8,128)S(1)}, u32[]{:S(2)}, u32[]{:S(2)}) collective-permute-start(f32[1,16,128]{2,1,0:T(8,128)S(1)} %get-tuple-element.600), channel_id=1, source_target_pairs={{4,0},{8,4},{12,8},{16,12},{20,16},{24,20},{28,24},{5,1},{9,5},{13... | collective-permute-start | bytes 24584 | tf_op jit(solution)/shard_map/while/body/eval_jaxpr/ppermute | solution.py:17
  156.7 32.3 %collective-permute-start.1 = (f32[1,16,128]{2,1,0:T(8,128)S(1)}, f32[1,16,128]{2,1,0:T(8,128)S(1)}, u32[]{:S(2)}, u32[]{:S(2)}) collective-permute-start(f32[1,16,128]{2,1,0:T(8,128)S(1)} %get-tuple-element.603), channel_id=1, source_target_pairs={{0,4},{4,8},{8,12},{12,16},{16,20},{20,24},{24,28},{1,5},{5,9},{9,... | collective-permute-start | bytes 24584 | tf_op jit(solution)/shard_map/while/body/eval_jaxpr/ppermute | solution.py:17
  160.9 16.2 %collective-permute-start.3 = (f32[5,128]{1,0:T(8,128)S(1)}, f32[5,128]{1,0:T(8,128)S(1)}, u32[]{:S(2)}, u32[]{:S(2)}) collective-permute-start(f32[5,128]{1,0:T(8,128)S(1)} %pad_maximum_fusion.8), channel_id=1, source_target_pairs={{0,1},{1,2},{2,3},{4,5},{5,6},{6,7},{8,9},{9,10},{10,11},{12,13},{... | collective-permute-start | bytes 7688 | tf_op jit(solution)/shard_map/while/body/eval_jaxpr/ppermute | solution.py:17
  189.2 33.6 %collective-permute-start = (f32[1,16,128]{2,1,0:T(8,128)S(1)}, f32[1,16,128]{2,1,0:T(8,128)S(1)}, u32[]{:S(2)}, u32[]{:S(2)}) collective-permute-start(f32[1,16,128]{2,1,0:T(8,128)S(1)} %get-tuple-element.600), channel_id=1, source_target_pairs={{4,0},{8,4},{12,8},{16,12},{20,16},{24,20},{28,24},{5,1},{9,5},{13... | collective-permute-start | bytes 24584 | tf_op jit(solution)/shard_map/while/body/eval_jaxpr/ppermute | solution.py:17
  190.5 32.3 %collective-permute-start.1 = (f32[1,16,128]{2,1,0:T(8,128)S(1)}, f32[1,16,128]{2,1,0:T(8,128)S(1)}, u32[]{:S(2)}, u32[]{:S(2)}) collective-permute-start(f32[1,16,128]{2,1,0:T(8,128)S(1)} %get-tuple-element.603), channel_id=1, source_target_pairs={{0,4},{4,8},{8,12},{12,16},{16,20},{20,24},{24,28},{1,5},{5,9},{9,... | collective-permute-start | bytes 24584 | tf_op jit(solution)/shard_map/while/body/eval_jaxpr/ppermute | solution.py:17
  194.7 16.2 %collective-permute-start.3 = (f32[5,128]{1,0:T(8,128)S(1)}, f32[5,128]{1,0:T(8,128)S(1)}, u32[]{:S(2)}, u32[]{:S(2)}) collective-permute-start(f32[5,128]{1,0:T(8,128)S(1)} %pad_maximum_fusion.8), channel_id=1, source_target_pairs={{0,1},{1,2},{2,3},{4,5},{5,6},{6,7},{8,9},{9,10},{10,11},{12,13},{... | collective-permute-start | bytes 7688 | tf_op jit(solution)/shard_map/while/body/eval_jaxpr/ppermute | solution.py:17
  222.9 33.6 %collective-permute-start = (f32[1,16,128]{2,1,0:T(8,128)S(1)}, f32[1,16,128]{2,1,0:T(8,128)S(1)}, u32[]{:S(2)}, u32[]{:S(2)}) collective-permute-start(f32[1,16,128]{2,1,0:T(8,128)S(1)} %get-tuple-element.600), channel_id=1, source_target_pairs={{4,0},{8,4},{12,8},{16,12},{20,16},{24,20},{28,24},{5,1},{9,5},{13... | collective-permute-start | bytes 24584 | tf_op jit(solution)/shard_map/while/body/eval_jaxpr/ppermute | solution.py:17
  224.2 32.3 %collective-permute-start.1 = (f32[1,16,128]{2,1,0:T(8,128)S(1)}, f32[1,16,128]{2,1,0:T(8,128)S(1)}, u32[]{:S(2)}, u32[]{:S(2)}) collective-permute-start(f32[1,16,128]{2,1,0:T(8,128)S(1)} %get-tuple-element.603), channel_id=1, source_target_pairs={{0,4},{4,8},{8,12},{12,16},{16,20},{20,24},{24,28},{1,5},{5,9},{9,... | collective-permute-start | bytes 24584 | tf_op jit(solution)/shard_map/while/body/eval_jaxpr/ppermute | solution.py:17
  228.5 16.2 %collective-permute-start.3 = (f32[5,128]{1,0:T(8,128)S(1)}, f32[5,128]{1,0:T(8,128)S(1)}, u32[]{:S(2)}, u32[]{:S(2)}) collective-permute-start(f32[5,128]{1,0:T(8,128)S(1)} %pad_maximum_fusion.8), channel_id=1, source_target_pairs={{0,1},{1,2},{2,3},{4,5},{5,6},{6,7},{8,9},{9,10},{10,11},{12,13},{... | collective-permute-start | bytes 7688 | tf_op jit(solution)/shard_map/while/body/eval_jaxpr/ppermute | solution.py:17
  231.4 13.4 %collective-permute-start.2 = (f32[5,128]{1,0:T(8,128)S(1)}, f32[5,128]{1,0:T(8,128)S(1)}, u32[]{:S(2)}, u32[]{:S(2)}) collective-permute-start(f32[5,128]{1,0:T(8,128)S(1)} %pad_maximum_fusion.7), channel_id=1, source_target_pairs={{1,0},{2,1},{3,2},{5,4},{6,5},{7,6},{9,8},{10,9},{11,10},{13,12},{... | collective-permute-start | bytes 7688 | tf_op jit(solution)/shard_map/while/body/eval_jaxpr/ppermute | solution.py:17
  256.7 33.6 %collective-permute-start = (f32[1,16,128]{2,1,0:T(8,128)S(1)}, f32[1,16,128]{2,1,0:T(8,128)S(1)}, u32[]{:S(2)}, u32[]{:S(2)}) collective-permute-start(f32[1,16,128]{2,1,0:T(8,128)S(1)} %get-tuple-element.600), channel_id=1, source_target_pairs={{4,0},{8,4},{12,8},{16,12},{20,16},{24,20},{28,24},{5,1},{9,5},{13... | collective-permute-start | bytes 24584 | tf_op jit(solution)/shard_map/while/body/eval_jaxpr/ppermute | solution.py:17
  258.0 32.3 %collective-permute-start.1 = (f32[1,16,128]{2,1,0:T(8,128)S(1)}, f32[1,16,128]{2,1,0:T(8,128)S(1)}, u32[]{:S(2)}, u32[]{:S(2)}) collective-permute-start(f32[1,16,128]{2,1,0:T(8,128)S(1)} %get-tuple-element.603), channel_id=1, source_target_pairs={{0,4},{4,8},{8,12},{12,16},{16,20},{20,24},{24,28},{1,5},{5,9},{9,... | collective-permute-start | bytes 24584 | tf_op jit(solution)/shard_map/while/body/eval_jaxpr/ppermute | solution.py:17
  262.2 16.2 %collective-permute-start.3 = (f32[5,128]{1,0:T(8,128)S(1)}, f32[5,128]{1,0:T(8,128)S(1)}, u32[]{:S(2)}, u32[]{:S(2)}) collective-permute-start(f32[5,128]{1,0:T(8,128)S(1)} %pad_maximum_fusion.8), channel_id=1, source_target_pairs={{0,1},{1,2},{2,3},{4,5},{5,6},{6,7},{8,9},{9,10},{10,11},{12,13},{... | collective-permute-start | bytes 7688 | tf_op jit(solution)/shard_map/while/body/eval_jaxpr/ppermute | solution.py:17
  265.2 13.4 %collective-permute-start.2 = (f32[5,128]{1,0:T(8,128)S(1)}, f32[5,128]{1,0:T(8,128)S(1)}, u32[]{:S(2)}, u32[]{:S(2)}) collective-permute-start(f32[5,128]{1,0:T(8,128)S(1)} %pad_maximum_fusion.7), channel_id=1, source_target_pairs={{1,0},{2,1},{3,2},{5,4},{6,5},{7,6},{9,8},{10,9},{11,10},{13,12},{... | collective-permute-start | bytes 7688 | tf_op jit(solution)/shard_map/while/body/eval_jaxpr/ppermute | solution.py:17
  290.5 33.6 %collective-permute-start = (f32[1,16,128]{2,1,0:T(8,128)S(1)}, f32[1,16,128]{2,1,0:T(8,128)S(1)}, u32[]{:S(2)}, u32[]{:S(2)}) collective-permute-start(f32[1,16,128]{2,1,0:T(8,128)S(1)} %get-tuple-element.600), channel_id=1, source_target_pairs={{4,0},{8,4},{12,8},{16,12},{20,16},{24,20},{28,24},{5,1},{9,5},{13... | collective-permute-start | bytes 24584 | tf_op jit(solution)/shard_map/while/body/eval_jaxpr/ppermute | solution.py:17
  291.8 32.3 %collective-permute-start.1 = (f32[1,16,128]{2,1,0:T(8,128)S(1)}, f32[1,16,128]{2,1,0:T(8,128)S(1)}, u32[]{:S(2)}, u32[]{:S(2)}) collective-permute-start(f32[1,16,128]{2,1,0:T(8,128)S(1)} %get-tuple-element.603), channel_id=1, source_target_pairs={{0,4},{4,8},{8,12},{12,16},{16,20},{20,24},{24,28},{1,5},{5,9},{9,... | collective-permute-start | bytes 24584 | tf_op jit(solution)/shard_map/while/body/eval_jaxpr/ppermute | solution.py:17
  296.0 16.2 %collective-permute-start.3 = (f32[5,128]{1,0:T(8,128)S(1)}, f32[5,128]{1,0:T(8,128)S(1)}, u32[]{:S(2)}, u32[]{:S(2)}) collective-permute-start(f32[5,128]{1,0:T(8,128)S(1)} %pad_maximum_fusion.8), channel_id=1, source_target_pairs={{0,1},{1,2},{2,3},{4,5},{5,6},{6,7},{8,9},{9,10},{10,11},{12,13},{... | collective-permute-start | bytes 7688 | tf_op jit(solution)/shard_map/while/body/eval_jaxpr/ppermute | solution.py:17
  324.2 33.6 %collective-permute-start = (f32[1,16,128]{2,1,0:T(8,128)S(1)}, f32[1,16,128]{2,1,0:T(8,128)S(1)}, u32[]{:S(2)}, u32[]{:S(2)}) collective-permute-start(f32[1,16,128]{2,1,0:T(8,128)S(1)} %get-tuple-element.600), channel_id=1, source_target_pairs={{4,0},{8,4},{12,8},{16,12},{20,16},{24,20},{28,24},{5,1},{9,5},{13... | collective-permute-start | bytes 24584 | tf_op jit(solution)/shard_map/while/body/eval_jaxpr/ppermute | solution.py:17
  325.5 32.3 %collective-permute-start.1 = (f32[1,16,128]{2,1,0:T(8,128)S(1)}, f32[1,16,128]{2,1,0:T(8,128)S(1)}, u32[]{:S(2)}, u32[]{:S(2)}) collective-permute-start(f32[1,16,128]{2,1,0:T(8,128)S(1)} %get-tuple-element.603), channel_id=1, source_target_pairs={{0,4},{4,8},{8,12},{12,16},{16,20},{20,24},{24,28},{1,5},{5,9},{9,... | collective-permute-start | bytes 24584 | tf_op jit(solution)/shard_map/while/body/eval_jaxpr/ppermute | solution.py:17
  329.8 16.2 %collective-permute-start.3 = (f32[5,128]{1,0:T(8,128)S(1)}, f32[5,128]{1,0:T(8,128)S(1)}, u32[]{:S(2)}, u32[]{:S(2)}) collective-permute-start(f32[5,128]{1,0:T(8,128)S(1)} %pad_maximum_fusion.8), channel_id=1, source_target_pairs={{0,1},{1,2},{2,3},{4,5},{5,6},{6,7},{8,9},{9,10},{10,11},{12,13},{... | collective-permute-start | bytes 7688 | tf_op jit(solution)/shard_map/while/body/eval_jaxpr/ppermute | solution.py:17
  358.0 33.6 %collective-permute-start = (f32[1,16,128]{2,1,0:T(8,128)S(1)}, f32[1,16,128]{2,1,0:T(8,128)S(1)}, u32[]{:S(2)}, u32[]{:S(2)}) collective-permute-start(f32[1,16,128]{2,1,0:T(8,128)S(1)} %get-tuple-element.600), channel_id=1, source_target_pairs={{4,0},{8,4},{12,8},{16,12},{20,16},{24,20},{28,24},{5,1},{9,5},{13... | collective-permute-start | bytes 24584 | tf_op jit(solution)/shard_map/while/body/eval_jaxpr/ppermute | solution.py:17
  359.3 32.3 %collective-permute-start.1 = (f32[1,16,128]{2,1,0:T(8,128)S(1)}, f32[1,16,128]{2,1,0:T(8,128)S(1)}, u32[]{:S(2)}, u32[]{:S(2)}) collective-permute-start(f32[1,16,128]{2,1,0:T(8,128)S(1)} %get-tuple-element.603), channel_id=1, source_target_pairs={{0,4},{4,8},{8,12},{12,16},{16,20},{20,24},{24,28},{1,5},{5,9},{9,... | collective-permute-start | bytes 24584 | tf_op jit(solution)/shard_map/while/body/eval_jaxpr/ppermute | solution.py:17
  363.5 16.2 %collective-permute-start.3 = (f32[5,128]{1,0:T(8,128)S(1)}, f32[5,128]{1,0:T(8,128)S(1)}, u32[]{:S(2)}, u32[]{:S(2)}) collective-permute-start(f32[5,128]{1,0:T(8,128)S(1)} %pad_maximum_fusion.8), channel_id=1, source_target_pairs={{0,1},{1,2},{2,3},{4,5},{5,6},{6,7},{8,9},{9,10},{10,11},{12,13},{... | collective-permute-start | bytes 7688 | tf_op jit(solution)/shard_map/while/body/eval_jaxpr/ppermute | solution.py:17
  391.8 33.6 %collective-permute-start = (f32[1,16,128]{2,1,0:T(8,128)S(1)}, f32[1,16,128]{2,1,0:T(8,128)S(1)}, u32[]{:S(2)}, u32[]{:S(2)}) collective-permute-start(f32[1,16,128]{2,1,0:T(8,128)S(1)} %get-tuple-element.600), channel_id=1, source_target_pairs={{4,0},{8,4},{12,8},{16,12},{20,16},{24,20},{28,24},{5,1},{9,5},{13... | collective-permute-start | bytes 24584 | tf_op jit(solution)/shard_map/while/body/eval_jaxpr/ppermute | solution.py:17
  393.1 32.3 %collective-permute-start.1 = (f32[1,16,128]{2,1,0:T(8,128)S(1)}, f32[1,16,128]{2,1,0:T(8,128)S(1)}, u32[]{:S(2)}, u32[]{:S(2)}) collective-permute-start(f32[1,16,128]{2,1,0:T(8,128)S(1)} %get-tuple-element.603), channel_id=1, source_target_pairs={{0,4},{4,8},{8,12},{12,16},{16,20},{20,24},{24,28},{1,5},{5,9},{9,... | collective-permute-start | bytes 24584 | tf_op jit(solution)/shard_map/while/body/eval_jaxpr/ppermute | solution.py:17
  397.3 16.2 %collective-permute-start.3 = (f32[5,128]{1,0:T(8,128)S(1)}, f32[5,128]{1,0:T(8,128)S(1)}, u32[]{:S(2)}, u32[]{:S(2)}) collective-permute-start(f32[5,128]{1,0:T(8,128)S(1)} %pad_maximum_fusion.8), channel_id=1, source_target_pairs={{0,1},{1,2},{2,3},{4,5},{5,6},{6,7},{8,9},{9,10},{10,11},{12,13},{... | collective-permute-start | bytes 7688 | tf_op jit(solution)/shard_map/while/body/eval_jaxpr/ppermute | solution.py:17
  425.5 33.6 %collective-permute-start = (f32[1,16,128]{2,1,0:T(8,128)S(1)}, f32[1,16,128]{2,1,0:T(8,128)S(1)}, u32[]{:S(2)}, u32[]{:S(2)}) collective-permute-start(f32[1,16,128]{2,1,0:T(8,128)S(1)} %get-tuple-element.600), channel_id=1, source_target_pairs={{4,0},{8,4},{12,8},{16,12},{20,16},{24,20},{28,24},{5,1},{9,5},{13... | collective-permute-start | bytes 24584 | tf_op jit(solution)/shard_map/while/body/eval_jaxpr/ppermute | solution.py:17
  426.8 32.3 %collective-permute-start.1 = (f32[1,16,128]{2,1,0:T(8,128)S(1)}, f32[1,16,128]{2,1,0:T(8,128)S(1)}, u32[]{:S(2)}, u32[]{:S(2)}) collective-permute-start(f32[1,16,128]{2,1,0:T(8,128)S(1)} %get-tuple-element.603), channel_id=1, source_target_pairs={{0,4},{4,8},{8,12},{12,16},{16,20},{20,24},{24,28},{1,5},{5,9},{9,... | collective-permute-start | bytes 24584 | tf_op jit(solution)/shard_map/while/body/eval_jaxpr/ppermute | solution.py:17
  431.1 16.2 %collective-permute-start.3 = (f32[5,128]{1,0:T(8,128)S(1)}, f32[5,128]{1,0:T(8,128)S(1)}, u32[]{:S(2)}, u32[]{:S(2)}) collective-permute-start(f32[5,128]{1,0:T(8,128)S(1)} %pad_maximum_fusion.8), channel_id=1, source_target_pairs={{0,1},{1,2},{2,3},{4,5},{5,6},{6,7},{8,9},{9,10},{10,11},{12,13},{... | collective-permute-start | bytes 7688 | tf_op jit(solution)/shard_map/while/body/eval_jaxpr/ppermute | solution.py:17
  459.3 33.6 %collective-permute-start = (f32[1,16,128]{2,1,0:T(8,128)S(1)}, f32[1,16,128]{2,1,0:T(8,128)S(1)}, u32[]{:S(2)}, u32[]{:S(2)}) collective-permute-start(f32[1,16,128]{2,1,0:T(8,128)S(1)} %get-tuple-element.600), channel_id=1, source_target_pairs={{4,0},{8,4},{12,8},{16,12},{20,16},{24,20},{28,24},{5,1},{9,5},{13... | collective-permute-start | bytes 24584 | tf_op jit(solution)/shard_map/while/body/eval_jaxpr/ppermute | solution.py:17
  460.6 32.3 %collective-permute-start.1 = (f32[1,16,128]{2,1,0:T(8,128)S(1)}, f32[1,16,128]{2,1,0:T(8,128)S(1)}, u32[]{:S(2)}, u32[]{:S(2)}) collective-permute-start(f32[1,16,128]{2,1,0:T(8,128)S(1)} %get-tuple-element.603), channel_id=1, source_target_pairs={{0,4},{4,8},{8,12},{12,16},{16,20},{20,24},{24,28},{1,5},{5,9},{9,... | collective-permute-start | bytes 24584 | tf_op jit(solution)/shard_map/while/body/eval_jaxpr/ppermute | solution.py:17
  464.8 16.2 %collective-permute-start.3 = (f32[5,128]{1,0:T(8,128)S(1)}, f32[5,128]{1,0:T(8,128)S(1)}, u32[]{:S(2)}, u32[]{:S(2)}) collective-permute-start(f32[5,128]{1,0:T(8,128)S(1)} %pad_maximum_fusion.8), channel_id=1, source_target_pairs={{0,1},{1,2},{2,3},{4,5},{5,6},{6,7},{8,9},{9,10},{10,11},{12,13},{... | collective-permute-start | bytes 7688 | tf_op jit(solution)/shard_map/while/body/eval_jaxpr/ppermute | solution.py:17
  (97 other events, 695.5 us)
